TPU v7x, 32 devices: a whole 2x2x4 slice. The times are simulated.
32 devices in a mesh: bulk: 4 (over x, core), grid: 8 (over z, y).
Axes of the slice: x: 2, y: 2, z: 4, core: 2. Of those that a mesh axis runs over, the one named last changes fastest.
Arguments:
- offsets: float32 [8, 3, 4, 24, 128], P('grid', None, 'bulk'), may hold values from -0.75 to 0.75
- flow: float32 [8, 5, 4, 24, 128], P('grid', None, 'bulk'), may hold values from -6 to 6
- control_points: float32 [3, 16384], P(None, ('bulk', 'grid')), may hold values from -7 to 13
- rbf_weights: float32 [3, 16384], P(None, ('bulk', 'grid')), may hold values from -2 to 2
- peer_offset: int32 [8, 720, 1], P('grid', 'bulk'), may hold values from 0 to 6; in each aligned block of 180 rows (0 to 179, 180 to 359, ..., all dimensions but the last counted through in order) at most 28 rows name the same one
- donor_block: int32 [8, 720], P('grid', 'bulk'), may hold values from 0 to 23
- receptor_block: int32 [8, 720], P('grid', 'bulk'), may hold values from 0 to 23
Outputs:
- moved: float32 [8, 3, 4, 24, 128], P('grid', None, 'bulk')
- metric: float32 [8, 4, 24, 128], P('grid', 'bulk')
- fringe: float32 [8, 5, 4, 24, 128], P('grid', None, 'bulk')
Inputs may be any that keep to these rules, and one draw needn't show every extreme that they name: `peer_offset`: in the 180 rows of one device no value appears more than 28 times.
All inputs are finite; a program needn't handle non-finite values.
Results may differ from a plain program's by a relative error of at most 0.0003.
Values sent between devices are 32-bit elements; how exact they have to be, the bound alone decides.
A program may use at most 64 MiB of HBM per device.

v0:
```python
import math
import jax
import jax.numpy as jnp
from jax import lax
from jax.sharding import PartitionSpec as P

CAP = 28
HIGHEST = lax.Precision.HIGHEST
SUPPORT = 1.25
point_block = 2048


def padded_2(cells, sides, width):
    for axis, dim in sides:
        count = lax.axis_size(axis)
        head = lax.slice_in_dim(cells, 0, width, axis=dim)
        tail = lax.slice_in_dim(cells, cells.shape[dim] - width, cells.shape[dim], axis=dim)
        cells = jnp.concatenate(
            [
                lax.ppermute(tail, axis, [(i, (i + 1) % count) for i in range(count)]),
                cells,
                lax.ppermute(head, axis, [((i + 1) % count, i) for i in range(count)]),
            ],
            axis=dim,
        )
    return cells


def lattice(grid_ids, plane_ids, planes_total, radial, lines):
    theta = 2.0 * math.pi * plane_ids.astype(jnp.float32) / planes_total
    radius = 1.0 + 0.25 * jnp.arange(radial, dtype=jnp.float32)
    height = 0.1 * jnp.arange(lines, dtype=jnp.float32)
    centre = 0.5 * grid_ids.astype(jnp.float32)
    xcoord = (
        centre[:, None, None, None]
        + radius[None, None, :, None] * jnp.cos(theta)[None, :, None, None]
        + 0.0 * height[None, None, None, :]
    )
    ycoord = (radius[None, :, None] * jnp.sin(theta)[:, None, None] + 0.0 * height[None, None, :])[
        None
    ] + 0.0 * centre[:, None, None, None]
    zcoord = jnp.zeros_like(xcoord) + height[None, None, None, :]
    return jnp.stack([xcoord, ycoord, zcoord], axis=1)


def kernel_sum(nodes, points, weights):
    squared = (nodes[0][:, None] - points[0][None, :]) ** 2
    squared = squared + (nodes[1][:, None] - points[1][None, :]) ** 2
    squared = squared + (nodes[2][:, None] - points[2][None, :]) ** 2
    scaled = jnp.sqrt(squared) / SUPPORT
    inside = jnp.maximum(1.0 - scaled, 0.0)
    basis = inside**4 * (4.0 * scaled + 1.0)
    return jnp.einsum("ck,nk->cn", weights, basis, precision=HIGHEST)


def deck_terms(carry, nodes, points, weights):
    breadth = points.shape[1]
    tile_width = math.gcd(breadth, point_block)
    turns = breadth // tile_width

    def one_tile(tile_number, running):
        tile_points = lax.dynamic_slice_in_dim(points, tile_number * tile_width, tile_width, 1)
        tile_weights = lax.dynamic_slice_in_dim(weights, tile_number * tile_width, tile_width, 1)
        return running + kernel_sum(nodes, tile_points, tile_weights)

    return lax.fori_loop(0, turns, one_tile, carry)


def along_axis(field, axis):
    total = field.shape[axis]
    ahead = lax.slice_in_dim(field, 2, total, axis=axis)
    behind = lax.slice_in_dim(field, 0, total - 2, axis=axis)
    first = lax.slice_in_dim(field, 1, 2, axis=axis) - lax.slice_in_dim(field, 0, 1, axis=axis)
    last = lax.slice_in_dim(field, total - 1, total, axis=axis) - lax.slice_in_dim(
        field, total - 2, total - 1, axis=axis
    )
    return jnp.concatenate([first, (ahead - behind) * 0.5, last], axis=axis)


def jacobian(slope_plane, slope_radial, slope_height):
    cross_x = slope_radial[:, 1] * slope_height[:, 2] - slope_radial[:, 2] * slope_height[:, 1]
    cross_y = slope_radial[:, 2] * slope_height[:, 0] - slope_radial[:, 0] * slope_height[:, 2]
    cross_z = slope_radial[:, 0] * slope_height[:, 1] - slope_radial[:, 1] * slope_height[:, 0]
    return slope_plane[:, 0] * cross_x + slope_plane[:, 1] * cross_y + slope_plane[:, 2] * cross_z


def blend(receptor_xyz, donor_xyz, donor_values):
    squared = (receptor_xyz[:, 0, :, None] - donor_xyz[:, 0, None, :]) ** 2
    squared = squared + (receptor_xyz[:, 1, :, None] - donor_xyz[:, 1, None, :]) ** 2
    squared = squared + (receptor_xyz[:, 2, :, None] - donor_xyz[:, 2, None, :]) ** 2
    weight = 1.0 / (0.25 + squared)
    totals = jnp.sum(weight, axis=2)
    weighted = jnp.einsum("nad,nvd->nva", weight, donor_values, precision=HIGHEST)
    return weighted / totals[:, None, :]


def blend_group(items):
    receptor_xyz, donor = items
    return blend(receptor_xyz, donor[:, :3], donor[:, 3:])


def local(offsets, flow, control_points, rbf_weights, peer_offset, donor_block, receptor_block):
    planes = offsets.shape[2]
    radial = offsets.shape[3]
    lines = offsets.shape[4]
    blocks = planes * radial
    grids = lax.axis_size("grid")
    grid_here = lax.axis_index("grid")
    plane_ids = lax.axis_index("bulk") * planes + jnp.arange(planes, dtype=jnp.int32)
    base = (
        lattice(grid_here[None], plane_ids, planes * lax.axis_size("bulk"), radial, lines) + offsets
    )
    nodes = base[0].reshape(3, -1)
    empty = jnp.zeros(nodes.shape, jnp.float32)
    all_points, all_weights = (
        lax.all_gather(control_points, ("bulk", "grid"), axis=1, tiled=True),
        lax.all_gather(rbf_weights, ("bulk", "grid"), axis=1, tiled=True),
    )
    shifts = deck_terms(empty, nodes, all_points, all_weights)
    moved = base + shifts.reshape(base.shape)
    padded = padded_2(moved, (("bulk", 2),), 1)
    slope_plane = (padded[:, :, 2:] - padded[:, :, :-2]) * 0.5
    slope_radial = along_axis(moved, 3)
    slope_height = along_axis(moved, 4)
    metric = jacobian(slope_plane, slope_radial, slope_height)
    values = metric[:, None] * flow
    payload = jnp.concatenate([moved, values], axis=1)[0].reshape(-1, blocks, lines)
    coords = moved[0].reshape(3, blocks, lines)
    block_iota = jnp.arange(blocks, dtype=jnp.int32)
    pick_donor = (donor_block[0][:, None] == block_iota[None, :]).astype(jnp.float32)
    chosen = jnp.einsum("sb,cbk->sck", pick_donor, payload, precision=HIGHEST)
    receiver = (grid_here + 1 + peer_offset[0, :, 0]) % grids
    receiver_hot = (receiver[:, None] == jnp.arange(grids, dtype=jnp.int32)[None, :]).astype(
        jnp.int32
    )
    before = jnp.cumsum(receiver_hot, axis=0) - receiver_hot
    position = jnp.sum(before * receiver_hot, axis=1)
    capacity = CAP
    target = receiver * capacity + position
    place = (jnp.arange(grids * capacity, dtype=jnp.int32)[:, None] == target[None, :]).astype(
        jnp.float32
    )
    label = (receptor_block[0] + 1).astype(jnp.float32)
    label_sent = jnp.einsum("ts,s->t", place, label, precision=HIGHEST).reshape(grids, capacity)
    sent = jnp.einsum("ts,sck->tck", place, chosen, precision=HIGHEST).reshape(
        grids, capacity, -1, lines
    )
    arrived, arrived_label = (
        lax.all_to_all(sent, "grid", split_axis=0, concat_axis=0, tiled=True),
        lax.all_to_all(label_sent, "grid", split_axis=0, concat_axis=0, tiled=True),
    )
    pick_receptor = (
        arrived_label.reshape(-1)[:, None] == (block_iota + 1).astype(jnp.float32)[None, :]
    ).astype(jnp.float32)
    receptor_xyz = jnp.einsum("tb,cbk->tck", pick_receptor, coords, precision=HIGHEST).reshape(
        grids, capacity, 3, lines
    )
    interpolated = lax.map(blend_group, (receptor_xyz, arrived)).reshape(
        grids * capacity, -1, lines
    )
    fringe = jnp.einsum("tb,tvk->vbk", pick_receptor, interpolated, precision=HIGHEST)
    return (moved, metric, fringe.reshape(1, -1, planes, radial, lines))


def solution(mesh):
    in_specs = (
        P("grid", None, "bulk", None, None),
        P("grid", None, "bulk", None, None),
        P(None, ("bulk", "grid")),
        P(None, ("bulk", "grid")),
        P("grid", "bulk", None),
        P("grid", "bulk"),
        P("grid", "bulk"),
    )
    out_specs = (
        P("grid", None, "bulk", None, None),
        P("grid", "bulk", None, None),
        P("grid", None, "bulk", None, None),
    )
    return jax.shard_map(local, mesh=mesh, in_specs=in_specs, out_specs=out_specs, check_vma=False)
```

profile of v0, /device:TPU:0, one launch (start us, length us, event | category | flops | bytes accessed | tf_op | source)
XLA Modules:
  0.0 534.4 jit_solution(6957581617032053949)
XLA Ops:
  1.7 71.5 %all_gather.7 = f32[3,16384]{1,0:T(4,128)S(1)} all-gather(f32[3,512]{1,0:T(4,128)} %param.13), channel_id=1, replica_groups=mesh['bulk'=4,'grid'=8] {'bulk','grid'}, dimensions={1}, use_global_device_ids=true | all-gather | bytes 202752 | tf_op jit(solution)/shard_map/all_gather | solution.py:116
  73.2 65.0 %all_gather.6 = f32[3,16384]{1,0:T(4,128)S(1)} all-gather(f32[3,512]{1,0:T(4,128)} %param.14), channel_id=1, replica_groups=mesh['bulk'=4,'grid'=8] {'bulk','grid'}, dimensions={1}, use_global_device_ids=true | all-gather | bytes 202752 | tf_op jit(solution)/shard_map/all_gather | solution.py:117
  138.2 300.2 %while.27 = (s32[]{:T(128)}, f32[3,3072]{1,0:T(4,128)S(1)}, f32[3,16384]{1,0:T(4,128)S(1)}, f32[3,3072]{1,0:T(4,128)S(1)}, f32[3,16384]{1,0:T(4,128)S(1)}, /*ind...) while((s32[]{:T(128)}, f32[3,3072]{1,0:T(4,128)S(1)}, ...), condition=%wide.region_1.0_spmd.clone, body=%wide.region_0.0_spmd.clone.sunk | while | flops 327174144 | bytes 303317 | solution.py:66
  138.3 37.3 %fusion.98 = f32[3,3072]{1,0:T(4,128)S(1)} fusion(f32[2048]{0:T(1024)S(1)} %bitcast.128, f32[3072]{0:T(1024)S(1)} %bitcast.124, f32[2048]{0:T(1024)S(1)} %bitcast.127, f32[3072]{0:T(1024)S(1)} %bitcast.125, f32[2048]{0:T(1024)S(1)} %bitcast.126, f32[3072]{0:T(1024)S(1)} %bitcast.123, f32[3,3072]{1,0:T(4,128)S(1)} %get-tuple-element.325, ...), kind=kOutput, calls=%fused_computation.44.clone.1 | convolution fusion | flops 327174144 | bytes 180229 | tf_op jit(solution)/shard_map/while/body/eval_jaxpr/ck,nk->cn/dot_general | solution.py:53
  175.8 37.3 %fusion.98 = f32[3,3072]{1,0:T(4,128)S(1)} fusion(f32[2048]{0:T(1024)S(1)} %bitcast.128, f32[3072]{0:T(1024)S(1)} %bitcast.124, f32[2048]{0:T(1024)S(1)} %bitcast.127, f32[3072]{0:T(1024)S(1)} %bitcast.125, f32[2048]{0:T(1024)S(1)} %bitcast.126, f32[3072]{0:T(1024)S(1)} %bitcast.123, f32[3,3072]{1,0:T(4,128)S(1)} %get-tuple-element.325, ...), kind=kOutput, calls=%fused_computation.44.clone.1 | convolution fusion | flops 327174144 | bytes 180229 | tf_op jit(solution)/shard_map/while/body/eval_jaxpr/ck,nk->cn/dot_general | solution.py:53
  213.3 37.3 %fusion.98 = f32[3,3072]{1,0:T(4,128)S(1)} fusion(f32[2048]{0:T(1024)S(1)} %bitcast.128, f32[3072]{0:T(1024)S(1)} %bitcast.124, f32[2048]{0:T(1024)S(1)} %bitcast.127, f32[3072]{0:T(1024)S(1)} %bitcast.125, f32[2048]{0:T(1024)S(1)} %bitcast.126, f32[3072]{0:T(1024)S(1)} %bitcast.123, f32[3,3072]{1,0:T(4,128)S(1)} %get-tuple-element.325, ...), kind=kOutput, calls=%fused_computation.44.clone.1 | convolution fusion | flops 327174144 | bytes 180229 | tf_op jit(solution)/shard_map/while/body/eval_jaxpr/ck,nk->cn/dot_general | solution.py:53
  250.8 37.3 %fusion.98 = f32[3,3072]{1,0:T(4,128)S(1)} fusion(f32[2048]{0:T(1024)S(1)} %bitcast.128, f32[3072]{0:T(1024)S(1)} %bitcast.124, f32[2048]{0:T(1024)S(1)} %bitcast.127, f32[3072]{0:T(1024)S(1)} %bitcast.125, f32[2048]{0:T(1024)S(1)} %bitcast.126, f32[3072]{0:T(1024)S(1)} %bitcast.123, f32[3,3072]{1,0:T(4,128)S(1)} %get-tuple-element.325, ...), kind=kOutput, calls=%fused_computation.44.clone.1 | convolution fusion | flops 327174144 | bytes 180229 | tf_op jit(solution)/shard_map/while/body/eval_jaxpr/ck,nk->cn/dot_general | solution.py:53
  288.3 37.3 %fusion.98 = f32[3,3072]{1,0:T(4,128)S(1)} fusion(f32[2048]{0:T(1024)S(1)} %bitcast.128, f32[3072]{0:T(1024)S(1)} %bitcast.124, f32[2048]{0:T(1024)S(1)} %bitcast.127, f32[3072]{0:T(1024)S(1)} %bitcast.125, f32[2048]{0:T(1024)S(1)} %bitcast.126, f32[3072]{0:T(1024)S(1)} %bitcast.123, f32[3,3072]{1,0:T(4,128)S(1)} %get-tuple-element.325, ...), kind=kOutput, calls=%fused_computation.44.clone.1 | convolution fusion | flops 327174144 | bytes 180229 | tf_op jit(solution)/shard_map/while/body/eval_jaxpr/ck,nk->cn/dot_general | solution.py:53
  325.8 37.3 %fusion.98 = f32[3,3072]{1,0:T(4,128)S(1)} fusion(f32[2048]{0:T(1024)S(1)} %bitcast.128, f32[3072]{0:T(1024)S(1)} %bitcast.124, f32[2048]{0:T(1024)S(1)} %bitcast.127, f32[3072]{0:T(1024)S(1)} %bitcast.125, f32[2048]{0:T(1024)S(1)} %bitcast.126, f32[3072]{0:T(1024)S(1)} %bitcast.123, f32[3,3072]{1,0:T(4,128)S(1)} %get-tuple-element.325, ...), kind=kOutput, calls=%fused_computation.44.clone.1 | convolution fusion | flops 327174144 | bytes 180229 | tf_op jit(solution)/shard_map/while/body/eval_jaxpr/ck,nk->cn/dot_general | solution.py:53
  363.3 37.3 %fusion.98 = f32[3,3072]{1,0:T(4,128)S(1)} fusion(f32[2048]{0:T(1024)S(1)} %bitcast.128, f32[3072]{0:T(1024)S(1)} %bitcast.124, f32[2048]{0:T(1024)S(1)} %bitcast.127, f32[3072]{0:T(1024)S(1)} %bitcast.125, f32[2048]{0:T(1024)S(1)} %bitcast.126, f32[3072]{0:T(1024)S(1)} %bitcast.123, f32[3,3072]{1,0:T(4,128)S(1)} %get-tuple-element.325, ...), kind=kOutput, calls=%fused_computation.44.clone.1 | convolution fusion | flops 327174144 | bytes 180229 | tf_op jit(solution)/shard_map/while/body/eval_jaxpr/ck,nk->cn/dot_general | solution.py:53
  400.8 37.3 %fusion.98 = f32[3,3072]{1,0:T(4,128)S(1)} fusion(f32[2048]{0:T(1024)S(1)} %bitcast.128, f32[3072]{0:T(1024)S(1)} %bitcast.124, f32[2048]{0:T(1024)S(1)} %bitcast.127, f32[3072]{0:T(1024)S(1)} %bitcast.125, f32[2048]{0:T(1024)S(1)} %bitcast.126, f32[3072]{0:T(1024)S(1)} %bitcast.123, f32[3,3072]{1,0:T(4,128)S(1)} %get-tuple-element.325, ...), kind=kOutput, calls=%fused_computation.44.clone.1 | convolution fusion | flops 327174144 | bytes 180229 | tf_op jit(solution)/shard_map/while/body/eval_jaxpr/ck,nk->cn/dot_general | solution.py:53
  442.3 3.5 all-to-all-start.1
  448.9 3.3 all-to-all-done.1
  452.2 3.6 all-to-all-start
  457.5 19.4 %all-to-all-done = f32[8,28,8,128]{3,2,1,0:T(8,128)S(1)} async-done(((f32[8,28,8,128]{3,2,1,0:T(8,128)}), f32[8,28,8,128]{3,2,1,0:T(8,128)S(1)}, u32[]{:S(2)}, u32[]{:S(2)}) %all-to-all-start) | async-done | bytes 917536 | tf_op jit(solution)/shard_map/all_to_all | solution.py:149
  476.9 56.5 %while.26 = (s32[]{:T(128)}, f32[8,28,5,128]{3,2,1,0:T(8,128)S(1)}, f32[8,28,8,128]{3,2,1,0:T(8,128)S(1)}, f32[8,28,3,128]{3,1,2,0:T(8,128)S(1)}, s32[]{:T(128)}) while((s32[]{:T(128)}, f32[8,28,5,128]{3,2,1,0:T(8,128)S(1)}, f32[8,28,8,128]{3,2,1,0:T(8,128)S(1)}, f32[8,28,3,128]{3,1,2,0:T(8,128)S(1)}, s32[]{:T(128)}) %tuple.87), condition=%wide.region_7.8_spmd, body=%wide.region_5.7_spmd.sunk | while | flops 37173248 | bytes 1017937 | solution.py:158
  479.4 4.5 fusion.94
  486.5 4.5 fusion.94
  493.5 4.5 fusion.94
  500.6 4.5 fusion.94
  507.7 4.5 fusion.94
  514.7 4.5 fusion.94
  521.8 4.5 fusion.94
  528.9 4.5 fusion.94
  (123 shorter events, 31.6 us)
Async XLA Ops:
  138.2 300.2 %copy-start.1 = (f32[1,3,1,24,128]{4,3,2,1,0:T(8,128)S(1)}, f32[1,3,1,24,128]{4,3,2,1,0:T(8,128)}, u32[]{:S(2)}) copy-start(f32[1,3,1,24,128]{4,3,2,1,0:T(8,128)} %param.11) | copy-start | bytes 110596
  138.2 302.1 %copy-start.5 = (s32[1,180,1]{1,2,0:T(1,128)S(1)}, s32[1,180,1]{1,2,0:T(1,128)}, u32[]{:S(2)}) copy-start(s32[1,180,1]{1,2,0:T(1,128)} %param.15) | copy-start | bytes 2164
  138.2 303.1 %copy-start.6 = (s32[1,180]{1,0:T(1,128)S(1)}, s32[1,180]{1,0:T(1,128)}, u32[]{:S(2)}) copy-start(s32[1,180]{1,0:T(1,128)} %param.17) | copy-start | bytes 2164
  438.4 7.8 %copy-start.2 = (f32[1,5,1,24,128]{4,3,2,1,0:T(8,128)S(1)}, f32[1,5,1,24,128]{4,3,2,1,0:T(8,128)}, u32[]{:S(2)}) copy-start(f32[1,5,1,24,128]{4,3,2,1,0:T(8,128)} %param.12) | copy-start | bytes 184324
  438.4 7.8 %copy-start.4 = (s32[1,180]{1,0:T(1,128)S(1)}, s32[1,180]{1,0:T(1,128)}, u32[]{:S(2)}) copy-start(s32[1,180]{1,0:T(1,128)} %param.16) | copy-start | bytes 2164
  438.4 18.6 %copy-start = (f32[1,3,1,24,128]{4,3,1,2,0:T(8,128)}, f32[1,3,1,24,128]{4,3,1,2,0:T(8,128)S(1)}, u32[]{:S(2)}) copy-start(f32[1,3,1,24,128]{4,3,1,2,0:T(8,128)S(1)} %bitcast_add_fusion) | copy-start | bytes 110596
  438.4 7.7 %collective-permute-start.1 = (f32[1,3,1,24,128]{4,3,1,2,0:T(8,128)S(1)}, f32[1,3,1,24,128]{4,3,1,2,0:T(8,128)S(1)}, u32[]{:S(2)}, u32[]{:S(2)}) collective-permute-start(f32[1,3,1,24,128]{4,3,1,2,0:T(8,128)S(1)} %bitcast_add_fusion), channel_id=1, source_target_pairs={{0,8},{8,16},{16,24},{24,0},{1,9},{9,17},{17,25},{25,1},{2,10},{10... | collective-permute-start | bytes 110600 | tf_op jit(solution)/shard_map/ppermute | solution.py:20
  438.5 7.6 %collective-permute-start = (f32[1,3,1,24,128]{4,3,1,2,0:T(8,128)S(1)}, f32[1,3,1,24,128]{4,3,1,2,0:T(8,128)S(1)}, u32[]{:S(2)}, u32[]{:S(2)}) collective-permute-start(f32[1,3,1,24,128]{4,3,1,2,0:T(8,128)S(1)} %bitcast_add_fusion), channel_id=1, source_target_pairs={{8,0},{16,8},{24,16},{0,24},{9,1},{17,9},{25,17},{1,25},{10,2},{18... | collective-permute-start | bytes 110600 | tf_op jit(solution)/shard_map/ppermute | solution.py:22
  442.3 9.9 %all-to-all-start.1 = ((f32[8,1,28]{2,1,0:T(1,128)}), f32[8,1,28]{2,1,0:T(1,128)S(1)}, u32[]{:S(2)}, u32[]{:S(2)}) async-start(f32[8,1,28]{2,1,0:T(1,128)} %convolution_bitcast_fusion.1), calls=%async_computation.1 | async-start | bytes 8192 | tf_op jit(solution)/shard_map/all_to_all | solution.py:150
  446.2 1.2 copy-start.3
  452.2 24.7 %all-to-all-start = ((f32[8,28,8,128]{3,2,1,0:T(8,128)}), f32[8,28,8,128]{3,2,1,0:T(8,128)S(1)}, u32[]{:S(2)}, u32[]{:S(2)}) async-start(f32[8,28,8,128]{3,2,1,0:T(8,128)} %bitcast.19), calls=%async_computation | async-start | bytes 1835008 | tf_op jit(solution)/shard_map/all_to_all | solution.py:149
where the time goes:
time: 535 us; the launch traced here: 534 us
  matrix products  339 us (63%)
  blocking collectives  136 us (25%)
  waiting for transfers between devices  22.7 us (4%)
  other arithmetic  22.2 us (4%)
  starting transfers between devices  8.83 us (2%)
    dot_general x8, matrix products, kernel_sum(): return jnp.einsum('ck,nk->cn', weights, basis, precision=HIGHEST)  299 us
    all_gather x1, blocking collectives, local(): lax.all_gather(control_points, ('bulk', 'grid'), axis=1, tiled=True)  71.5 us
    all_gather x1, blocking collectives, local(): lax.all_gather(rbf_weights, ('bulk', 'grid'), axis=1, tiled=True)  65 us
    dot_general x8, matrix products, blend(): jnp.einsum('nad,nvd->nva', weight, donor_values, precision=HIGHEST)  36.2 us
    reduce_sum x8, other arithmetic, blend(): totals = jnp.sum(weight, axis=2)  19.5 us
    all_to_all x1, waiting for transfers between devices, local(): lax.all_to_all(sent, 'grid', split_axis=0, concat_axis=0, tiled=True)  19.4 us
  transfers between devices with their start and end apart: 4, of which 2 were waited for; matrix products, arithmetic and copies ran while one was open for 1% of the time, Pallas kernels for 0%

commit v1 on v0

--- a/solution.py
+++ b/solution.py
@@ -8,6 +8,30 @@
 HIGHEST = lax.Precision.HIGHEST
 SUPPORT = 1.25
 point_block = 2048
+
+
+def map_wall(arr, k_dim):
+    oldest = list(arr.shape[1:])
+    oldest[k_dim] *= arr.shape[0]
+    return jnp.moveaxis(arr, 0, k_dim).reshape(oldest)
+
+
+def load_the_seats_all(arr_in, device_axis):
+    full_n = lax.axis_size(device_axis)
+    parts_out = arr_in[None]
+    for at in range(full_n.bit_length() - 1):
+        long_array = 1 << at
+        then = lax.ppermute(
+            parts_out, axis_name=device_axis, perm=[(s, s ^ long_array) for s in range(full_n)]
+        )
+        aux = jnp.stack([parts_out, then], 0)
+        current_block = lax.axis_index(device_axis) >> at & 1
+        parts_out = jnp.where(current_block == 0, aux, aux[::-1]).reshape(-1, *arr_in.shape)
+    return parts_out
+
+
+def tell_spans(s0, incoming_x, which_dim):
+    return map_wall(load_the_seats_all(s0, incoming_x), which_dim)
 
 
 def padded_2(cells, sides, width):
@@ -114,7 +138,7 @@
     empty = jnp.zeros(nodes.shape, jnp.float32)
     all_points, all_weights = (
         lax.all_gather(control_points, ("bulk", "grid"), axis=1, tiled=True),
-        lax.all_gather(rbf_weights, ("bulk", "grid"), axis=1, tiled=True),
+        tell_spans(rbf_weights, ("bulk", "grid"), 1),
     )
     shifts = deck_terms(empty, nodes, all_points, all_weights)
     moved = base + shifts.reshape(base.shape)

time: 535 us -> 489 us (0.914)
  blocking collectives: 136 us -> 69.3 us
  starting transfers between devices: 8.83 us -> 21.5 us
  waiting for transfers between devices: 22.7 us -> 30.1 us
    all_gather x1 -> x0, blocking collectives: 65 us -> none  [local(): lax.all_gather(rbf_weights, ('bulk', 'grid'), axis=1, tiled=True)]
    ppermute x0 -> x5, starting transfers between devices: none -> 8.86 us  [load_the_seats_all(): lax.ppermute(parts_out, axis_name=device_axis, perm=[(s, s ^ long_array)...]
    ppermute x0 -> x5, waiting for transfers between devices: none -> 6.44 us  [load_the_seats_all(): lax.ppermute(parts_out, axis_name=device_axis, perm=[(s, s ^ long_array)...]
  transfers between devices with their start and end apart: 4 -> 9, of which waited for: 2 -> 6; matrix products, arithmetic and copies ran while one was open for 1% -> 62% of each run, Pallas kernels for 0% -> 0%
where the time goes in v1:
time: 489 us
  matrix products  339 us (69%)
  blocking collectives  69.3 us (14%)
  waiting for transfers between devices  30.1 us (6%)
  other arithmetic  22.9 us (5%)
  starting transfers between devices  21.5 us (4%)
    dot_general x8, matrix products, kernel_sum(): return jnp.einsum('ck,nk->cn', weights, basis, precision=HIGHEST)  299 us
    all_gather x1, blocking collectives, local(): lax.all_gather(control_points, ('bulk', 'grid'), axis=1, tiled=True)  69.3 us
    dot_general x8, matrix products, blend(): jnp.einsum('nad,nvd->nva', weight, donor_values, precision=HIGHEST)  36.2 us
    all_to_all x1, waiting for transfers between devices, local(): lax.all_to_all(sent, 'grid', split_axis=0, concat_axis=0, tiled=True)  22.2 us
    reduce_sum x8, other arithmetic, blend(): totals = jnp.sum(weight, axis=2)  19.5 us
  transfers between devices with their start and end apart: 9, of which 6 were waited for; matrix products, arithmetic and copies ran while one was open for 62% of the time, Pallas kernels for 0%

profile of v1, /device:TPU:0, one launch (start us, length us, event | category | flops | bytes accessed | tf_op | source)
XLA Modules:
  0.0 489.0 jit_solution(6064156811481585679)
XLA Ops:
  4.1 7.3 %all-to-all-start.1 = ((f32[8,1,28]{2,1,0:T(1,128)}), f32[8,1,28]{2,1,0:T(1,128)S(1)}, u32[]{:S(2)}, u32[]{:S(2)}) async-start(f32[8,1,28]{2,1,0:T(1,128)} %convolution_bitcast_fusion.1), calls=%async_computation.1 | async-start | bytes 8192 | tf_op jit(solution)/shard_map/all_to_all | solution.py:174
  19.8 3.1 collective-permute-start.2
  27.9 69.3 %all_gather.3 = f32[3,16384]{1,0:T(4,128)S(1)} all-gather(f32[3,512]{1,0:T(4,128)S(1)} %copy-done.4), channel_id=1, replica_groups=mesh['bulk'=4,'grid'=8] {'bulk','grid'}, dimensions={1}, use_global_device_ids=true | all-gather | bytes 202752 | tf_op jit(solution)/shard_map/all_gather | solution.py:140
  97.4 300.2 %while.27 = (s32[]{:T(128)}, f32[3,3072]{1,0:T(4,128)S(1)}, f32[3,16384]{1,0:T(4,128)S(1)}, f32[3,3072]{1,0:T(4,128)S(1)}, f32[3,16384]{1,0:T(4,128)S(1)}, /*ind...) while((s32[]{:T(128)}, f32[3,3072]{1,0:T(4,128)S(1)}, ...), condition=%wide.region_1.2_spmd.clone, body=%wide.region_0.1_spmd.clone.sunk | while | flops 327174144 | bytes 303317 | solution.py:90
  97.6 37.3 %fusion.100 = f32[3,3072]{1,0:T(4,128)S(1)} fusion(f32[2048]{0:T(1024)S(1)} %bitcast.159, f32[3072]{0:T(1024)S(1)} %bitcast.152, f32[2048]{0:T(1024)S(1)} %bitcast.158, f32[3072]{0:T(1024)S(1)} %bitcast.153, f32[2048]{0:T(1024)S(1)} %bitcast.157, f32[3072]{0:T(1024)S(1)} %bitcast.151, f32[3,3072]{1,0:T(4,128)S(1)} %get-tuple-element.329, ...), kind=kOutput, calls=%fused_computation.44.clone.1 | convolution fusion | flops 327174144 | bytes 180229 | tf_op jit(solution)/shard_map/while/body/eval_jaxpr/ck,nk->cn/dot_general | solution.py:77
  135.1 37.3 %fusion.100 = f32[3,3072]{1,0:T(4,128)S(1)} fusion(f32[2048]{0:T(1024)S(1)} %bitcast.159, f32[3072]{0:T(1024)S(1)} %bitcast.152, f32[2048]{0:T(1024)S(1)} %bitcast.158, f32[3072]{0:T(1024)S(1)} %bitcast.153, f32[2048]{0:T(1024)S(1)} %bitcast.157, f32[3072]{0:T(1024)S(1)} %bitcast.151, f32[3,3072]{1,0:T(4,128)S(1)} %get-tuple-element.329, ...), kind=kOutput, calls=%fused_computation.44.clone.1 | convolution fusion | flops 327174144 | bytes 180229 | tf_op jit(solution)/shard_map/while/body/eval_jaxpr/ck,nk->cn/dot_general | solution.py:77
  172.6 37.3 %fusion.100 = f32[3,3072]{1,0:T(4,128)S(1)} fusion(f32[2048]{0:T(1024)S(1)} %bitcast.159, f32[3072]{0:T(1024)S(1)} %bitcast.152, f32[2048]{0:T(1024)S(1)} %bitcast.158, f32[3072]{0:T(1024)S(1)} %bitcast.153, f32[2048]{0:T(1024)S(1)} %bitcast.157, f32[3072]{0:T(1024)S(1)} %bitcast.151, f32[3,3072]{1,0:T(4,128)S(1)} %get-tuple-element.329, ...), kind=kOutput, calls=%fused_computation.44.clone.1 | convolution fusion | flops 327174144 | bytes 180229 | tf_op jit(solution)/shard_map/while/body/eval_jaxpr/ck,nk->cn/dot_general | solution.py:77
  210.1 37.3 %fusion.100 = f32[3,3072]{1,0:T(4,128)S(1)} fusion(f32[2048]{0:T(1024)S(1)} %bitcast.159, f32[3072]{0:T(1024)S(1)} %bitcast.152, f32[2048]{0:T(1024)S(1)} %bitcast.158, f32[3072]{0:T(1024)S(1)} %bitcast.153, f32[2048]{0:T(1024)S(1)} %bitcast.157, f32[3072]{0:T(1024)S(1)} %bitcast.151, f32[3,3072]{1,0:T(4,128)S(1)} %get-tuple-element.329, ...), kind=kOutput, calls=%fused_computation.44.clone.1 | convolution fusion | flops 327174144 | bytes 180229 | tf_op jit(solution)/shard_map/while/body/eval_jaxpr/ck,nk->cn/dot_general | solution.py:77
  247.6 37.3 %fusion.100 = f32[3,3072]{1,0:T(4,128)S(1)} fusion(f32[2048]{0:T(1024)S(1)} %bitcast.159, f32[3072]{0:T(1024)S(1)} %bitcast.152, f32[2048]{0:T(1024)S(1)} %bitcast.158, f32[3072]{0:T(1024)S(1)} %bitcast.153, f32[2048]{0:T(1024)S(1)} %bitcast.157, f32[3072]{0:T(1024)S(1)} %bitcast.151, f32[3,3072]{1,0:T(4,128)S(1)} %get-tuple-element.329, ...), kind=kOutput, calls=%fused_computation.44.clone.1 | convolution fusion | flops 327174144 | bytes 180229 | tf_op jit(solution)/shard_map/while/body/eval_jaxpr/ck,nk->cn/dot_general | solution.py:77
  285.1 37.3 %fusion.100 = f32[3,3072]{1,0:T(4,128)S(1)} fusion(f32[2048]{0:T(1024)S(1)} %bitcast.159, f32[3072]{0:T(1024)S(1)} %bitcast.152, f32[2048]{0:T(1024)S(1)} %bitcast.158, f32[3072]{0:T(1024)S(1)} %bitcast.153, f32[2048]{0:T(1024)S(1)} %bitcast.157, f32[3072]{0:T(1024)S(1)} %bitcast.151, f32[3,3072]{1,0:T(4,128)S(1)} %get-tuple-element.329, ...), kind=kOutput, calls=%fused_computation.44.clone.1 | convolution fusion | flops 327174144 | bytes 180229 | tf_op jit(solution)/shard_map/while/body/eval_jaxpr/ck,nk->cn/dot_general | solution.py:77
  322.6 37.3 %fusion.100 = f32[3,3072]{1,0:T(4,128)S(1)} fusion(f32[2048]{0:T(1024)S(1)} %bitcast.159, f32[3072]{0:T(1024)S(1)} %bitcast.152, f32[2048]{0:T(1024)S(1)} %bitcast.158, f32[3072]{0:T(1024)S(1)} %bitcast.153, f32[2048]{0:T(1024)S(1)} %bitcast.157, f32[3072]{0:T(1024)S(1)} %bitcast.151, f32[3,3072]{1,0:T(4,128)S(1)} %get-tuple-element.329, ...), kind=kOutput, calls=%fused_computation.44.clone.1 | convolution fusion | flops 327174144 | bytes 180229 | tf_op jit(solution)/shard_map/while/body/eval_jaxpr/ck,nk->cn/dot_general | solution.py:77
  360.1 37.3 %fusion.100 = f32[3,3072]{1,0:T(4,128)S(1)} fusion(f32[2048]{0:T(1024)S(1)} %bitcast.159, f32[3072]{0:T(1024)S(1)} %bitcast.152, f32[2048]{0:T(1024)S(1)} %bitcast.158, f32[3072]{0:T(1024)S(1)} %bitcast.153, f32[2048]{0:T(1024)S(1)} %bitcast.157, f32[3072]{0:T(1024)S(1)} %bitcast.151, f32[3,3072]{1,0:T(4,128)S(1)} %get-tuple-element.329, ...), kind=kOutput, calls=%fused_computation.44.clone.1 | convolution fusion | flops 327174144 | bytes 180229 | tf_op jit(solution)/shard_map/while/body/eval_jaxpr/ck,nk->cn/dot_general | solution.py:77
  403.9 3.6 all-to-all-start
  409.2 22.2 %all-to-all-done = f32[8,28,8,128]{3,2,1,0:T(8,128)S(1)} async-done(((f32[8,28,8,128]{3,2,1,0:T(8,128)}), f32[8,28,8,128]{3,2,1,0:T(8,128)S(1)}, u32[]{:S(2)}, u32[]{:S(2)}) %all-to-all-start) | async-done | bytes 917536 | tf_op jit(solution)/shard_map/all_to_all | solution.py:173
  431.5 56.5 %while.26 = (s32[]{:T(128)}, f32[8,28,5,128]{3,2,1,0:T(8,128)S(1)}, f32[8,28,8,128]{3,2,1,0:T(8,128)S(1)}, f32[8,28,3,128]{3,1,2,0:T(8,128)S(1)}, s32[]{:T(128)}) while((s32[]{:T(128)}, f32[8,28,5,128]{3,2,1,0:T(8,128)S(1)}, f32[8,28,8,128]{3,2,1,0:T(8,128)S(1)}, f32[8,28,3,128]{3,1,2,0:T(8,128)S(1)}, s32[]{:T(128)}) %tuple.90), condition=%wide.region_7.8_spmd, body=%wide.region_5.7_spmd.sunk | while | flops 37173248 | bytes 1017937 | solution.py:182
  431.6 2.4 fusion.95
  434.0 4.5 fusion.96
  441.1 4.5 fusion.96
  448.1 4.5 fusion.96
  455.2 4.5 fusion.96
  462.3 4.5 fusion.96
  469.3 4.5 fusion.96
  476.4 4.5 fusion.96
  483.5 4.5 fusion.96
  (142 shorter events, 44.3 us)
Async XLA Ops:
  0.6 27.2 %copy-start.1 = (f32[1,3,1,24,128]{4,3,2,1,0:T(8,128)S(1)}, f32[1,3,1,24,128]{4,3,2,1,0:T(8,128)}, u32[]{:S(2)}) copy-start(f32[1,3,1,24,128]{4,3,2,1,0:T(8,128)} %param.11) | copy-start | bytes 110596
  0.6 27.3 %copy-start.4 = (f32[3,512]{1,0:T(4,128)S(1)}, f32[3,512]{1,0:T(4,128)}, u32[]{:S(2)}) copy-start(f32[3,512]{1,0:T(4,128)} %param.13) | copy-start | bytes 18436
  4.1 399.9 %all-to-all-start.1 = ((f32[8,1,28]{2,1,0:T(1,128)}), f32[8,1,28]{2,1,0:T(1,128)S(1)}, u32[]{:S(2)}, u32[]{:S(2)}) async-start(f32[8,1,28]{2,1,0:T(1,128)} %convolution_bitcast_fusion.1), calls=%async_computation.1 | async-start | bytes 8192 | tf_op jit(solution)/shard_map/all_to_all | solution.py:174
  11.4 3.9 collective-permute-start
  16.0 3.8 collective-permute-start.1
  19.8 5.0 %collective-permute-start.2 = (f32[4,3,512]{2,1,0:T(4,128)S(1)}, f32[4,3,512]{2,1,0:T(4,128)S(1)}, u32[]{:S(2)}, u32[]{:S(2)}) collective-permute-start(f32[4,3,512]{2,1,0:T(4,128)S(1)} %bitcast.160), channel_id=1, source_target_pairs={{0,4},{1,5},{2,6},{3,7},{4,0},{5,1},{6,2},{7,3},{8,12},{9,13},{10,... | collective-permute-start | bytes 73736 | tf_op jit(solution)/shard_map/ppermute | solution.py:24
  24.9 1.3 collective-permute-start.3
  26.3 70.9 %collective-permute-start.4 = (f32[16,3,512]{2,0,1:T(8,128)S(1)}, f32[16,3,512]{2,0,1:T(8,128)S(1)}, u32[]{:S(2)}, u32[]{:S(2)}) collective-permute-start(f32[16,3,512]{2,0,1:T(8,128)S(1)} %bitcast.148), channel_id=1, source_target_pairs={{0,16},{1,17},{2,18},{3,19},{4,20},{5,21},{6,22},{7,23},{8,24},{9,... | collective-permute-start | bytes 294920 | tf_op jit(solution)/shard_map/ppermute | solution.py:24
  397.6 3.6 copy-start.2
  397.6 3.6 copy-start.5
  397.7 11.1 %copy-start = (f32[1,3,1,24,128]{4,3,1,2,0:T(8,128)}, f32[1,3,1,24,128]{4,3,1,2,0:T(8,128)S(1)}, u32[]{:S(2)}) copy-start(f32[1,3,1,24,128]{4,3,1,2,0:T(8,128)S(1)} %bitcast_add_fusion) | copy-start | bytes 110596
  397.8 3.4 collective-permute-start.6
  397.8 3.4 collective-permute-start.5
  401.2 1.2 copy-start.3
  403.9 27.5 %all-to-all-start = ((f32[8,28,8,128]{3,2,1,0:T(8,128)}), f32[8,28,8,128]{3,2,1,0:T(8,128)S(1)}, u32[]{:S(2)}, u32[]{:S(2)}) async-start(f32[8,28,8,128]{3,2,1,0:T(8,128)} %bitcast.36), calls=%async_computation | async-start | bytes 1835008 | tf_op jit(solution)/shard_map/all_to_all | solution.py:173
